TPU v7x, 32 devices: a whole 2x2x4 slice. The times are simulated.
32 devices in a mesh: dp: 8 (over z, y), tensor: 4 (over x, core).
Axes of the slice: x: 2, y: 2, z: 4, core: 2. Of those that a mesh axis runs over, the one named last changes fastest.
Arguments:
- inputs: bfloat16 [608, 8, 1024], P('tensor', 'dp'), may hold values from -6 to 6
- attn_gain: bfloat16 [2, 1024], P(None, 'dp'), may hold values from 0.5 to 1.5
- attn_shift: bfloat16 [2, 1024], P(None, 'dp'), may hold values from -1.25 to 1.25
- qkv_weight: bfloat16 [2, 1024, 3, 1024], P(None, 'dp', None, 'tensor'), may hold values from -0.1875 to 0.1875
- query_bias: bfloat16 [2, 1024], P(None, 'dp'), may hold values from -3 to 3
- value_bias: bfloat16 [2, 1024], P(None, 'dp'), may hold values from -1.25 to 1.25
- out_weight: bfloat16 [2, 1024, 1024], P(None, 'tensor', 'dp'), may hold values from -2 to 2
- out_bias: bfloat16 [2, 1024], P(None, 'dp'), may hold values from -1.25 to 1.25
- mlp_gain: bfloat16 [2, 1024], P(None, 'dp'), may hold values from 0.5 to 1.5
- mlp_shift: bfloat16 [2, 1024], P(None, 'dp'), may hold values from -1.25 to 1.25
- up_weight: bfloat16 [2, 1024, 4096], P(None, 'dp', 'tensor'), may hold values from -0.1875 to 0.1875
- up_bias: bfloat16 [2, 4096], P(None, 'dp'), may hold values from -1.25 to 1.25
- down_weight: bfloat16 [2, 4096, 1024], P(None, 'tensor', 'dp'), may hold values from -0.09375 to 0.09375
- down_bias: bfloat16 [2, 1024], P(None, 'dp'), may hold values from -1.25 to 1.25
- cotangent: bfloat16 [608, 8, 1024], P('tensor', 'dp'), may hold values from -6 to 6
- image_mask: int32 [8], P('dp'), may hold values 0 or 1
- row_mask: int32 [608, 8], P(None, 'dp'), may hold values from 0 to 1, as said below
Outputs:
- outputs: bfloat16 [608, 8, 1024], P('tensor', 'dp')
- grad_inputs: float32 [608, 8, 1024], P('tensor', 'dp')
- grad_attn_gain: float32 [2, 1024], P(None, 'dp')
- grad_attn_shift: float32 [2, 1024], P(None, 'dp')
- grad_qkv_weight: float32 [2, 1024, 3, 1024], P(None, 'dp', None, 'tensor')
- grad_query_bias: float32 [2, 1024], P(None, 'dp')
- grad_value_bias: float32 [2, 1024], P(None, 'dp')
- grad_out_weight: float32 [2, 1024, 1024], P(None, 'tensor', 'dp')
- grad_out_bias: float32 [2, 1024], P(None, 'dp')
- grad_mlp_gain: float32 [2, 1024], P(None, 'dp')
- grad_mlp_shift: float32 [2, 1024], P(None, 'dp')
- grad_up_weight: float32 [2, 1024, 4096], P(None, 'dp', 'tensor')
- grad_up_bias: float32 [2, 4096], P(None, 'dp')
- grad_down_weight: float32 [2, 4096, 1024], P(None, 'tensor', 'dp')
- grad_down_bias: float32 [2, 1024], P(None, 'dp')
Inputs may be any that keep to these rules, and one draw needn't show every extreme that they name: `row_mask`: row 0 of every image is live; rows 577 and later are 0.
All inputs are finite; a program needn't handle non-finite values. No bound on the sum of `image_mask` on one device may be relied on, other than what follows from the above.
Results may differ from a plain program's by a relative error of at most 0.015.
Values may be sent and summed in bfloat16 or wider, within the bound.
A program may use at most 128 MiB of HBM per device.

v0:
```python
import jax
import jax.numpy as jnp
from jax import lax
from jax.sharding import PartitionSpec as P

HEAD_DIM = 64


def layer_norm(values, gain, shift):
    center = values - jnp.mean(values, -1, keepdims=True)
    inverse = lax.rsqrt(jnp.mean(center * center, -1, keepdims=True) + 1e-05)
    return center * inverse * gain + shift


def norm_backward(values, gain, grad_out):
    center = values - jnp.mean(values, -1, keepdims=True)
    inverse = lax.rsqrt(jnp.mean(center * center, -1, keepdims=True) + 1e-05)
    normal = center * inverse
    grad_hat = grad_out * gain
    grad_in = inverse * (
        grad_hat
        - jnp.mean(grad_hat, -1, keepdims=True)
        - normal * jnp.mean(grad_hat * normal, -1, keepdims=True)
    )
    return (grad_in, jnp.sum(grad_out * normal, (0, 1)), jnp.sum(grad_out, (0, 1)))


def quick_gelu(values):
    return values * jax.nn.sigmoid(1.702 * values)


def gelu_slope(values):
    sigma = jax.nn.sigmoid(1.702 * values)
    return sigma + 1.702 * values * sigma * (1.0 - sigma)


def image_scores(block, keep):
    scores = jnp.einsum(
        "qhe,khe->hqk", block[:, 0], block[:, 1], preferred_element_type=jnp.float32
    )
    scores = scores * HEAD_DIM ** (-0.5)
    return jnp.where(keep[None, None, :], scores, -1e30)


def attention_forward(qkv, row_mask):
    seq_len, images, width = (qkv.shape[0], qkv.shape[1], qkv.shape[3])
    heads = width // HEAD_DIM

    def one_image(which, carry):
        outs, lses = carry
        block = lax.dynamic_index_in_dim(qkv, which, 1, keepdims=False).reshape(
            seq_len, 3, heads, HEAD_DIM
        )
        keep = lax.dynamic_index_in_dim(row_mask, which, 1, keepdims=False) > 0
        scores = image_scores(block, keep)
        row_max = jnp.max(scores, -1, keepdims=True)
        expo = jnp.exp(scores - row_max)
        row_total = jnp.sum(expo, -1, keepdims=True)
        weights = (expo / row_total).astype(jnp.bfloat16)
        values = jnp.einsum(
            "hqk,khe->qhe", weights, block[:, 2], preferred_element_type=jnp.float32
        )
        values = values.astype(jnp.bfloat16).reshape(seq_len, 1, width)
        outs = values
        lses = lax.dynamic_update_index_in_dim(
            lses, (row_max + jnp.log(row_total))[:, :, 0], which, 0
        )
        return (outs, lses)

    start = (
        jnp.zeros((seq_len, images, width), jnp.bfloat16),
        jnp.zeros((images, heads, seq_len), jnp.float32),
    )
    return lax.fori_loop(0, images, one_image, start)


def attention_backward(qkv, lses, grad_mixed, row_mask):
    seq_len, images, width = (qkv.shape[0], qkv.shape[1], qkv.shape[3])
    heads = width // HEAD_DIM
    scale = HEAD_DIM ** (-0.5)

    def one_image(which, grads):
        block = lax.dynamic_index_in_dim(qkv, which, 1, keepdims=False).reshape(
            seq_len, 3, heads, HEAD_DIM
        )
        keep = lax.dynamic_index_in_dim(row_mask, which, 1, keepdims=False) > 0
        grad_out = lax.dynamic_index_in_dim(grad_mixed, which, 1, keepdims=False).reshape(
            seq_len, heads, HEAD_DIM
        )
        lse_here = lax.dynamic_index_in_dim(lses, which, 0, keepdims=False)
        weights = jnp.exp(image_scores(block, keep) - lse_here[:, :, None])
        grad_value = jnp.einsum(
            "hqk,qhe->khe",
            weights.astype(jnp.bfloat16),
            grad_out,
            preferred_element_type=jnp.float32,
        )
        grad_weights = jnp.einsum(
            "qhe,khe->hqk", grad_out, block[:, 2], preferred_element_type=jnp.float32
        )
        delta = jnp.sum(weights * grad_weights, -1, keepdims=True)
        grad_scores = (weights * (grad_weights - delta)).astype(jnp.bfloat16)
        grad_query = (
            jnp.einsum("hqk,khe->qhe", grad_scores, block[:, 1], preferred_element_type=jnp.float32)
            * scale
        )
        grad_key = (
            jnp.einsum("hqk,qhe->khe", grad_scores, block[:, 0], preferred_element_type=jnp.float32)
            * scale
        )
        stacked = jnp.stack([grad_query, grad_key, grad_value], 1).astype(jnp.bfloat16)
        return stacked.reshape(seq_len, 1, 3, width)

    return lax.fori_loop(0, images, one_image, jnp.zeros(qkv.shape, jnp.bfloat16))


def body(
    inputs,
    attn_gain,
    attn_shift,
    qkv_weight,
    query_bias,
    value_bias,
    out_weight,
    out_bias,
    mlp_gain,
    mlp_shift,
    up_weight,
    up_bias,
    down_weight,
    down_bias,
    cotangent,
    image_mask,
    row_mask,
):
    depth_count = qkv_weight.shape[0]
    tensor_rank = lax.axis_index("tensor")
    local_rows = inputs.shape[0]
    head_width = qkv_weight.shape[3]
    unit_width = up_weight.shape[2]
    vectors = jnp.stack(
        [attn_gain, attn_shift, query_bias, value_bias, out_bias, mlp_gain, mlp_shift, down_bias], 1
    )

    def fetch(depth):
        return (
            lax.all_gather(qkv_weight[depth], "dp", axis=0, tiled=True),
            lax.all_gather(up_weight[depth], "dp", axis=0, tiled=True),
            lax.all_gather(out_weight[depth], "dp", axis=1, tiled=True),
            lax.all_gather(down_weight[depth], "dp", axis=1, tiled=True),
            lax.all_gather(vectors[depth], "dp", axis=1, tiled=True),
            lax.all_gather(up_bias[depth], "dp", axis=0, tiled=True),
        )

    def unpack(weights):
        vec = weights[4].astype(jnp.float32)
        query_cols = lax.dynamic_slice_in_dim(vec[2], tensor_rank * head_width, head_width)
        value_cols = lax.dynamic_slice_in_dim(vec[3], tensor_rank * head_width, head_width)
        bias_three = jnp.stack([query_cols, jnp.zeros_like(query_cols), value_cols])
        up_cols = lax.dynamic_slice_in_dim(
            weights[5].astype(jnp.float32), tensor_rank * unit_width, unit_width
        )
        return (vec, bias_three, up_cols)

    def forward_parts(hidden, weights):
        qkv_w, up_w, out_w = (weights[0], weights[1], weights[2])
        vec, bias_three, up_cols = unpack(weights)
        normed = layer_norm(hidden, vec[0], vec[1]).astype(jnp.bfloat16)
        product = jnp.einsum(
            "sid,dce->sice",
            lax.all_gather(normed, "tensor", axis=0, tiled=True),
            qkv_w,
            preferred_element_type=jnp.float32,
        )
        qkv = (product + bias_three).astype(jnp.bfloat16)
        mixed, lses = attention_forward(qkv, row_mask)
        middle = (
            hidden
            + lax.psum_scatter(
                jnp.einsum("sie,ed->sid", mixed, out_w, preferred_element_type=jnp.float32).astype(
                    jnp.bfloat16
                ),
                "tensor",
                scatter_dimension=0,
                tiled=True,
            ).astype(jnp.float32)
            + vec[4]
        )
        normed_mid = layer_norm(middle, vec[5], vec[6]).astype(jnp.bfloat16)
        before = (
            jnp.einsum(
                "sid,df->sif",
                lax.all_gather(normed_mid, "tensor", axis=0, tiled=True),
                up_w,
                preferred_element_type=jnp.float32,
            )
            + up_cols
        )
        active = quick_gelu(before).astype(jnp.bfloat16)
        return (normed, qkv, mixed, lses, middle, normed_mid, before, active)

    hidden = inputs.astype(jnp.float32)
    kept = []
    layer_inputs = []
    stored = []
    for depth in range(depth_count):
        weights = fetch(depth)
        kept.append(weights)
        layer_inputs.append(hidden)
        parts = forward_parts(hidden, weights)
        stored.append(parts)
        down_cols = weights[4][7].astype(jnp.float32)
        mlp_active = parts[7]
        mlp_down_w = weights[3]
        hidden = (
            parts[4]
            + lax.psum_scatter(
                jnp.einsum(
                    "sif,fd->sid", mlp_active, mlp_down_w, preferred_element_type=jnp.float32
                ).astype(jnp.bfloat16),
                "tensor",
                scatter_dimension=0,
                tiled=True,
            ).astype(jnp.float32)
            + down_cols
        )
    live_rows = lax.dynamic_slice_in_dim(row_mask, tensor_rank * local_rows, local_rows, 0)
    live = (live_rows * image_mask[None, :]).astype(jnp.float32)
    grad = cotangent.astype(jnp.float32) * live[:, :, None]
    per_layer = []
    for depth in reversed(range(depth_count)):
        weights = kept[depth]
        parts = stored[depth]
        layer_qkv_w = weights[0]
        layer_up_w = weights[1]
        layer_out_w = weights[2]
        down_w = weights[3]
        layer_vec, layer_bias_three, layer_up_cols = unpack(weights)
        (
            layer_normed,
            layer_qkv,
            layer_mixed,
            layer_lses,
            layer_middle,
            layer_normed_mid,
            layer_before,
            layer_active,
        ) = parts
        full_width = layer_vec.shape[1]
        grad_down_bias = jnp.sum(grad, (0, 1))
        fold_piece = lax.all_gather(grad.astype(jnp.bfloat16), "tensor", axis=0, tiled=True)
        update = jnp.einsum("sid,fd->sif", fold_piece, down_w, preferred_element_type=jnp.float32)
        grad_down_w = jnp.einsum(
            "sif,sid->df", layer_active, fold_piece, preferred_element_type=jnp.float32
        )
        grad_before = (update * gelu_slope(layer_before)).astype(jnp.bfloat16)
        grad_up_cols = jnp.sum(grad_before.astype(jnp.float32), (0, 1))
        grad_up_w = jnp.einsum(
            "sid,sif->df",
            lax.all_gather(layer_normed_mid, "tensor", axis=0, tiled=True),
            grad_before,
            preferred_element_type=jnp.float32,
        )
        grad_normed_mid = lax.psum_scatter(
            jnp.einsum(
                "sif,df->sid", grad_before, layer_up_w, preferred_element_type=jnp.float32
            ).astype(jnp.bfloat16),
            "tensor",
            scatter_dimension=0,
            tiled=True,
        ).astype(jnp.float32)
        grad_mid, grad_mlp_gain, grad_mlp_shift = norm_backward(
            layer_middle, layer_vec[5], grad_normed_mid
        )
        grad_mid = grad_mid + grad
        grad_out_bias = jnp.sum(grad_mid, (0, 1))
        piece = lax.all_gather(grad_mid.astype(jnp.bfloat16), "tensor", axis=0, tiled=True)
        fold_update = jnp.einsum(
            "sid,ed->sie", piece, layer_out_w, preferred_element_type=jnp.float32
        )
        grad_out_w = jnp.einsum(
            "sie,sid->de", layer_mixed, piece, preferred_element_type=jnp.float32
        )
        grad_qkv = attention_backward(
            layer_qkv, layer_lses, fold_update.astype(jnp.bfloat16), row_mask
        )
        grad_bias_three = jnp.sum(grad_qkv.astype(jnp.float32), (0, 1))
        grad_qkv_w = jnp.einsum(
            "sid,sice->dce",
            lax.all_gather(layer_normed, "tensor", axis=0, tiled=True),
            grad_qkv,
            preferred_element_type=jnp.float32,
        )
        grad_normed = lax.psum_scatter(
            jnp.einsum(
                "sice,dce->sid", grad_qkv, layer_qkv_w, preferred_element_type=jnp.float32
            ).astype(jnp.bfloat16),
            "tensor",
            scatter_dimension=0,
            tiled=True,
        ).astype(jnp.float32)
        grad_in, grad_attn_gain, grad_attn_shift = norm_backward(
            layer_inputs[depth], layer_vec[0], grad_normed
        )
        grad_in = grad_in + grad_mid
        empty = jnp.zeros((full_width,), jnp.float32)
        grad_query = lax.dynamic_update_slice_in_dim(
            empty, grad_bias_three[0], tensor_rank * head_width, 0
        )
        grad_value = lax.dynamic_update_slice_in_dim(
            empty, grad_bias_three[2], tensor_rank * head_width, 0
        )
        grad_up_full = lax.dynamic_update_slice_in_dim(
            jnp.zeros((weights[5].shape[0],), jnp.float32),
            grad_up_cols,
            tensor_rank * unit_width,
            0,
        )
        grad_vec = jnp.stack(
            [
                grad_attn_gain,
                grad_attn_shift,
                grad_query,
                grad_value,
                grad_out_bias,
                grad_mlp_gain,
                grad_mlp_shift,
                grad_down_bias,
            ]
        )
        flat = jnp.concatenate(
            [grad_qkv_w.reshape(grad_qkv_w.shape[0], -1), grad_up_w, grad_out_w, grad_down_w], 1
        ).astype(jnp.bfloat16)
        flat = lax.psum_scatter(flat, "dp", scatter_dimension=0, tiled=True).astype(jnp.float32)
        ends = [3 * head_width, 3 * head_width + unit_width, 4 * head_width + unit_width]
        part_qkv, part_up, part_out, part_down = jnp.split(flat, ends, 1)
        shards = (
            part_qkv.reshape(-1, 3, head_width),
            part_up,
            part_out.T,
            part_down.T,
            grad_vec,
            grad_up_full,
        )
        grad = grad_in
        per_layer.insert(0, shards)
    vec_grads = jnp.stack([shards[4] for shards in per_layer])
    bias_grads = jnp.stack([shards[5] for shards in per_layer])
    whole_vec = jnp.concatenate([vec_grads, bias_grads.reshape(depth_count, -1, full_width)], 1)
    whole_vec = lax.psum(whole_vec, ("dp", "tensor"))
    dp_rank = lax.axis_index("dp")
    shard_width = attn_gain.shape[1]
    vec_sum = lax.dynamic_slice_in_dim(whole_vec[:, :8], dp_rank * shard_width, shard_width, 2)
    up_sum = lax.dynamic_slice_in_dim(
        whole_vec[:, 8:].reshape(depth_count, -1), dp_rank * up_bias.shape[1], up_bias.shape[1], 1
    )
    return (
        hidden.astype(jnp.bfloat16),
        grad,
        vec_sum[:, 0],
        vec_sum[:, 1],
        jnp.stack([shards[0] for shards in per_layer]),
        vec_sum[:, 2],
        vec_sum[:, 3],
        jnp.stack([shards[2] for shards in per_layer]),
        vec_sum[:, 4],
        vec_sum[:, 5],
        vec_sum[:, 6],
        jnp.stack([shards[1] for shards in per_layer]),
        up_sum,
        jnp.stack([shards[3] for shards in per_layer]),
        vec_sum[:, 7],
    )


def solution(mesh):
    in_specs = (
        P("tensor", "dp", None),
        P(None, "dp"),
        P(None, "dp"),
        P(None, "dp", None, "tensor"),
        P(None, "dp"),
        P(None, "dp"),
        P(None, "tensor", "dp"),
        P(None, "dp"),
        P(None, "dp"),
        P(None, "dp"),
        P(None, "dp", "tensor"),
        P(None, "dp"),
        P(None, "tensor", "dp"),
        P(None, "dp"),
        P("tensor", "dp", None),
        P("dp"),
        P(None, "dp"),
    )
    out_specs = (
        P("tensor", "dp", None),
        P("tensor", "dp", None),
        P(None, "dp"),
        P(None, "dp"),
        P(None, "dp", None, "tensor"),
        P(None, "dp"),
        P(None, "dp"),
        P(None, "tensor", "dp"),
        P(None, "dp"),
        P(None, "dp"),
        P(None, "dp"),
        P(None, "dp", "tensor"),
        P(None, "dp"),
        P(None, "tensor", "dp"),
        P(None, "dp"),
    )
    return jax.shard_map(body, mesh=mesh, in_specs=in_specs, out_specs=out_specs, check_vma=False)
```

profile of v0, /device:TPU:0, one launch (start us, length us, event | category | flops | bytes accessed | tf_op | source)
XLA Modules:
  0.0 1194.4 jit_solution(9559652890281156475)
XLA Ops:
  14.9 22.4 %all-gather = bf16[1,8,1024]{2,0,1:T(2,128)(2,1)S(1)} all-gather(bf16[1,8,128]{2,0,1:T(2,128)(2,1)S(1)} %get-tuple-element.196), channel_id=2, replica_groups=mesh['dp'=8,'tensor'=4] {'dp'}, dimensions={2}, use_global_device_ids=true | all-gather | bytes 18432 | tf_op jit(solution)/shard_map/all_gather | solution.py:151
  58.0 28.1 %all-gather.2 = bf16[1,256,1024]{2,1,0:T(8,128)(2,1)S(1)} all-gather(bf16[1,256,128]{2,1,0:T(8,128)(2,1)S(1)} %get-tuple-element.173), channel_id=4, replica_groups=mesh['dp'=8,'tensor'=4] {'dp'}, dimensions={2}, use_global_device_ids=true | all-gather | bytes 589824 | tf_op jit(solution)/shard_map/all_gather | solution.py:149
  114.5 24.1 %reduce-scatter.15.cloned.1.call-done = bf16[152,1,1024]{2,0,1:T(8,128)(2,1)} async-done(((bf16[608,1,1024]{2,0,1:T(8,128)(2,1)}), bf16[152,1,1024]{2,0,1:T(8,128)(2,1)}) %reduce-scatter.15.cloned.1.call-update) | async-done | bytes 311312 | tf_op jit(solution)/shard_map/reduce_scatter | solution.py:179
  143.8 26.2 %all-gather.4 = bf16[1,4096]{1,0:T(2,128)(2,1)S(1)} all-gather(bf16[1,512]{1,0:T(2,128)(2,1)S(1)} %get-tuple-element.199), channel_id=6, replica_groups=mesh['dp'=8,'tensor'=4] {'dp'}, dimensions={1}, use_global_device_ids=true | all-gather | bytes 9216 | tf_op jit(solution)/shard_map/all_gather | solution.py:152
  170.0 20.7 %all-gather.45.cloned.1.call-done = bf16[1,1024,1024]{2,1,0:T(8,128)(2,1)} async-done(((bf16[1,128,1024]{2,1,0:T(8,128)(2,1)}), bf16[1,1024,1024]{2,1,0:T(8,128)(2,1)}) %all-gather.45.cloned.1.call-update) | async-done | bytes 2097168 | tf_op jit(solution)/shard_map/all_gather | solution.py:148
  190.7 18.4 %all-gather.29.cloned.1.call-done = bf16[608,1,1024]{2,0,1:T(8,128)(2,1)} async-done(((bf16[152,1,1024]{2,0,1:T(8,128)(2,1)}), bf16[608,1,1024]{2,0,1:T(8,128)(2,1)}) %all-gather.29.cloned.1.call-update) | async-done | bytes 1245200 | tf_op jit(solution)/shard_map/all_gather | solution.py:193
  214.0 48.9 %all-gather.47.cloned.1.call-done = bf16[1,1024,1024]{2,1,0:T(8,128)(2,1)} async-done(((bf16[1,1024,128]{2,1,0:T(8,128)(2,1)}), bf16[1,1024,1024]{2,1,0:T(8,128)(2,1)}) %all-gather.47.cloned.1.call-update) | async-done | bytes 2097168 | tf_op jit(solution)/shard_map/all_gather | solution.py:150
  268.6 23.6 %reduce-scatter.17.cloned.1.call-done = bf16[152,1,1024]{2,0,1:T(8,128)(2,1)} async-done(((bf16[608,1,1024]{2,0,1:T(8,128)(2,1)}), bf16[152,1,1024]{2,0,1:T(8,128)(2,1)}) %reduce-scatter.17.cloned.1.call-update) | async-done | bytes 311312 | tf_op jit(solution)/shard_map/reduce_scatter | solution.py:217
  294.7 29.5 %all-gather.8 = bf16[1,256,1024]{2,1,0:T(8,128)(2,1)S(1)} all-gather(bf16[1,256,128]{2,1,0:T(8,128)(2,1)S(1)} %get-tuple-element.172), channel_id=10, replica_groups=mesh['dp'=8,'tensor'=4] {'dp'}, dimensions={2}, use_global_device_ids=true | all-gather | bytes 589824 | tf_op jit(solution)/shard_map/all_gather | solution.py:149
  341.1 18.8 %all-gather.31.cloned.1.call-done = bf16[608,1,1024]{2,0,1:T(8,128)(2,1)} async-done(((bf16[152,1,1024]{2,0,1:T(8,128)(2,1)}), bf16[608,1,1024]{2,0,1:T(8,128)(2,1)}) %all-gather.31.cloned.1.call-update) | async-done | bytes 1245200 | tf_op jit(solution)/shard_map/all_gather | solution.py:171
  376.5 25.5 %reduce-scatter.19.cloned.1.call-done = bf16[152,1,1024]{2,0,1:T(8,128)(2,1)} async-done(((bf16[608,1,1024]{2,0,1:T(8,128)(2,1)}), bf16[152,1,1024]{2,0,1:T(8,128)(2,1)}) %reduce-scatter.19.cloned.1.call-update) | async-done | bytes 311312 | tf_op jit(solution)/shard_map/reduce_scatter | solution.py:179
  406.6 26.2 %all-gather.10 = bf16[1,4096]{1,0:T(2,128)(2,1)S(1)} all-gather(bf16[1,512]{1,0:T(2,128)(2,1)S(1)} %get-tuple-element.198), channel_id=12, replica_groups=mesh['dp'=8,'tensor'=4] {'dp'}, dimensions={1}, use_global_device_ids=true | all-gather | bytes 9216 | tf_op jit(solution)/shard_map/all_gather | solution.py:152
  432.8 21.5 %all-gather.51.cloned.1.call-done = bf16[1,1024,1024]{2,1,0:T(8,128)(2,1)} async-done(((bf16[1,128,1024]{2,1,0:T(8,128)(2,1)}), bf16[1,1024,1024]{2,1,0:T(8,128)(2,1)}) %all-gather.51.cloned.1.call-update) | async-done | bytes 2097168 | tf_op jit(solution)/shard_map/all_gather | solution.py:148
  454.3 18.4 %all-gather.33.cloned.1.call-done = bf16[608,1,1024]{2,0,1:T(8,128)(2,1)} async-done(((bf16[152,1,1024]{2,0,1:T(8,128)(2,1)}), bf16[608,1,1024]{2,0,1:T(8,128)(2,1)}) %all-gather.33.cloned.1.call-update) | async-done | bytes 1245200 | tf_op jit(solution)/shard_map/all_gather | solution.py:193
  492.8 53.2 %all-gather.53.cloned.1.call-done = bf16[1,1024,1024]{2,1,0:T(8,128)(2,1)} async-done(((bf16[1,1024,128]{2,1,0:T(8,128)(2,1)}), bf16[1,1024,1024]{2,1,0:T(8,128)(2,1)}) %all-gather.53.cloned.1.call-update) | async-done | bytes 2097168 | tf_op jit(solution)/shard_map/all_gather | solution.py:150
  561.4 18.4 %reduce-scatter.23.cloned.1.call-done = bf16[152,1,1024]{2,0,1:T(8,128)(2,1)} async-done(((bf16[608,1,1024]{2,0,1:T(8,128)(2,1)}), bf16[152,1,1024]{2,0,1:T(8,128)(2,1)}) %reduce-scatter.23.cloned.1.call-update) | async-done | bytes 311312 | tf_op jit(solution)/shard_map/reduce_scatter | solution.py:264
  582.8 25.5 %reduce-scatter.21.cloned.1.call-done = bf16[152,1,1024]{2,0,1:T(8,128)(2,1)} async-done(((bf16[608,1,1024]{2,0,1:T(8,128)(2,1)}), bf16[152,1,1024]{2,0,1:T(8,128)(2,1)}) %reduce-scatter.21.cloned.1.call-update) | async-done | bytes 311312 | tf_op jit(solution)/shard_map/reduce_scatter | solution.py:217
  612.1 17.9 %all-gather.37.cloned.1.call-done = bf16[608,1,1024]{2,0,1:T(8,128)(2,1)} async-done(((bf16[152,1,1024]{2,0,1:T(8,128)(2,1)}), bf16[608,1,1024]{2,0,1:T(8,128)(2,1)}) %all-gather.37.cloned.1.call-update) | async-done | bytes 1245200 | tf_op jit(solution)/shard_map/all_gather | solution.py:277
  656.8 26.2 %reduce-scatter.25.cloned.1.call-done = bf16[152,1,1024]{2,0,1:T(8,128)(2,1)} async-done(((bf16[608,1,1024]{2,0,1:T(8,128)(2,1)}), bf16[152,1,1024]{2,0,1:T(8,128)(2,1)}) %reduce-scatter.25.cloned.1.call-update) | async-done | bytes 311312 | tf_op jit(solution)/shard_map/reduce_scatter | solution.py:294
  687.0 17.9 %all-gather.39.cloned.1.call-done = bf16[608,1,1024]{2,0,1:T(8,128)(2,1)} async-done(((bf16[152,1,1024]{2,0,1:T(8,128)(2,1)}), bf16[608,1,1024]{2,0,1:T(8,128)(2,1)}) %all-gather.39.cloned.1.call-update) | async-done | bytes 1245200 | tf_op jit(solution)/shard_map/all_gather | solution.py:251
  714.5 26.0 %reduce-scatter.27.cloned.1.call-done = bf16[152,1,1024]{2,0,1:T(8,128)(2,1)} async-done(((bf16[608,1,1024]{2,0,1:T(8,128)(2,1)}), bf16[152,1,1024]{2,0,1:T(8,128)(2,1)}) %reduce-scatter.27.cloned.1.call-update) | async-done | bytes 311312 | tf_op jit(solution)/shard_map/reduce_scatter | solution.py:264
  853.5 80.5 %all-reduce.2.cloned.1.call-done = f32[2,12,1024]{2,0,1:T(2,128)} async-done(((f32[2,12,1024]{2,0,1:T(2,128)}), f32[2,12,1024]{2,0,1:T(2,128)}) %all-reduce.2.cloned.1.call-update) | async-done | bytes 98320 | tf_op jit(solution)/shard_map/psum | solution.py:350
  936.7 119.5 %reduce-scatter.33.cloned.1.call-done = bf16[128,3072]{1,0:T(8,128)(2,1)} async-done(((bf16[1024,3072]{1,0:T(8,128)(2,1)}), bf16[128,3072]{1,0:T(8,128)(2,1)}) %reduce-scatter.33.cloned.1.call-update) | async-done | bytes 786448
  1059.7 117.3 %reduce-scatter.31.cloned.1.call-done = bf16[128,3072]{1,0:T(8,128)(2,1)} async-done(((bf16[1024,3072]{1,0:T(8,128)(2,1)}), bf16[128,3072]{1,0:T(8,128)(2,1)}) %reduce-scatter.31.cloned.1.call-update) | async-done | bytes 786448
  (383 shorter events, 323.5 us)
Async XLA Ops:
  7.2 78.9 %all-gather.27.cloned.1.call-start = ((), (), s32[]{:S(2)}) async-start(), calls=%async_computation.10 | async-start | bytes 1556480 | tf_op jit(solution)/shard_map/all_gather | solution.py:171
  39.3 63.6 %all-gather.43.cloned.1.call-start = ((), (), s32[]{:S(2)}) async-start(), calls=%async_computation.27 | async-start | bytes 1769472 | tf_op jit(solution)/shard_map/all_gather | solution.py:147
  41.2 97.4 %reduce-scatter.15.cloned.1.call-start = ((), (), s32[]{:S(2)}) async-start(), calls=%async_computation.11 | async-start | bytes 1556480 | tf_op jit(solution)/shard_map/reduce_scatter | solution.py:179
  113.5 77.2 %all-gather.45.cloned.1.call-start = ((), (), s32[]{:S(2)}) async-start(), calls=%async_computation.28 | async-start | bytes 2359296 | tf_op jit(solution)/shard_map/all_gather | solution.py:148
  114.4 94.7 %all-gather.29.cloned.1.call-start = ((), (), s32[]{:S(2)}) async-start(), calls=%async_computation.12 | async-start | bytes 1556480 | tf_op jit(solution)/shard_map/all_gather | solution.py:193
  142.9 120.0 %all-gather.47.cloned.1.call-start = ((), (), s32[]{:S(2)}) async-start(), calls=%async_computation.29 | async-start | bytes 2359296 | tf_op jit(solution)/shard_map/all_gather | solution.py:150
  143.8 148.5 %reduce-scatter.17.cloned.1.call-start = ((), (), s32[]{:S(2)}) async-start(), calls=%async_computation.13 | async-start | bytes 1556480 | tf_op jit(solution)/shard_map/reduce_scatter | solution.py:217
  267.8 73.3 %all-gather.49.cloned.1.call-start = ((), (), s32[]{:S(2)}) async-start(), calls=%async_computation.30 | async-start | bytes 1769472 | tf_op jit(solution)/shard_map/all_gather | solution.py:147
  268.6 91.4 %all-gather.31.cloned.1.call-start = ((), (), s32[]{:S(2)}) async-start(), calls=%async_computation.14 | async-start | bytes 1556480 | tf_op jit(solution)/shard_map/all_gather | solution.py:171
  294.7 107.4 %reduce-scatter.19.cloned.1.call-start = ((), (), s32[]{:S(2)}) async-start(), calls=%async_computation.15 | async-start | bytes 1556480 | tf_op jit(solution)/shard_map/reduce_scatter | solution.py:179
  375.8 78.6 %all-gather.51.cloned.1.call-start = ((), (), s32[]{:S(2)}) async-start(), calls=%async_computation.31 | async-start | bytes 2359296 | tf_op jit(solution)/shard_map/all_gather | solution.py:148
  376.5 96.3 %all-gather.33.cloned.1.call-start = ((), (), s32[]{:S(2)}) async-start(), calls=%async_computation.16 | async-start | bytes 1556480 | tf_op jit(solution)/shard_map/all_gather | solution.py:193
  404.3 88.5 %all-gather.35.cloned.1.call-start = ((), (), s32[]{:S(2)}) async-start(), calls=%async_computation.18 | async-start | bytes 1556480 | tf_op jit(solution)/shard_map/all_gather | solution.py:251
  406.0 140.0 %all-gather.53.cloned.1.call-start = ((), (), s32[]{:S(2)}) async-start(), calls=%async_computation.32 | async-start | bytes 2359296 | tf_op jit(solution)/shard_map/all_gather | solution.py:150
  406.6 173.2 %reduce-scatter.23.cloned.1.call-start = ((), (), s32[]{:S(2)}) async-start(), calls=%async_computation.19 | async-start | bytes 1556480 | tf_op jit(solution)/shard_map/reduce_scatter | solution.py:264
  555.3 53.0 %reduce-scatter.21.cloned.1.call-start = ((), (), s32[]{:S(2)}) async-start(), calls=%async_computation.17 | async-start | bytes 1556480 | tf_op jit(solution)/shard_map/reduce_scatter | solution.py:217
  560.3 69.7 %all-gather.37.cloned.1.call-start = ((), (), s32[]{:S(2)}) async-start(), calls=%async_computation.20 | async-start | bytes 1556480 | tf_op jit(solution)/shard_map/all_gather | solution.py:277
  612.0 71.0 %reduce-scatter.25.cloned.1.call-start = ((), (), s32[]{:S(2)}) async-start(), calls=%async_computation.21 | async-start | bytes 1556480 | tf_op jit(solution)/shard_map/reduce_scatter | solution.py:294
  687.0 53.5 %reduce-scatter.27.cloned.1.call-start = ((), (), s32[]{:S(2)}) async-start(), calls=%async_computation.23 | async-start | bytes 1556480 | tf_op jit(solution)/shard_map/reduce_scatter | solution.py:264
  714.2 48.9 %all-gather.41.cloned.1.call-start = ((), (), s32[]{:S(2)}) async-start(), calls=%async_computation.24 | async-start | bytes 1556480 | tf_op jit(solution)/shard_map/all_gather | solution.py:277
  745.2 62.0 %reduce-scatter.29.cloned.1.call-start = ((), (), s32[]{:S(2)}) async-start(), calls=%async_computation.25 | async-start | bytes 1556480 | tf_op jit(solution)/shard_map/reduce_scatter | solution.py:294
  780.9 153.0 %all-reduce.2.cloned.1.call-start = ((), (), s32[]{:S(2)}) async-start(), calls=%async_computation.26 | async-start | bytes 196608 | tf_op jit(solution)/shard_map/psum | solution.py:350
  809.5 246.7 %reduce-scatter.33.cloned.1.call-start = ((), (), s32[]{:S(2)}) async-start(), calls=%async_computation.34 | async-start | bytes 7077888
  824.0 352.9 %reduce-scatter.31.cloned.1.call-start = ((), (), s32[]{:S(2)}) async-start(), calls=%async_computation.33 | async-start | bytes 7077888
  (79 other events, 1483.6 us)
Sparse Core Ops, SparseCore 0:
  57.3 45.6 all-gather.42
  113.6 24.8 reduce-scatter.14
  141.3 49.3 all-gather.44
  192.8 16.2 all-gather.28
  211.8 51.0 all-gather.46
  267.9 24.2 reduce-scatter.16
  295.0 46.0 all-gather.48
  343.3 16.6 all-gather.30
  375.9 26.1 reduce-scatter.18
  405.0 49.3 all-gather.50
  456.4 16.2 all-gather.32
  475.0 17.8 all-gather.34
  494.9 51.0 all-gather.52
  555.4 24.2 reduce-scatter.22
  582.2 26.1 reduce-scatter.20
  612.1 17.8 all-gather.36
  656.8 26.1 reduce-scatter.24
  687.1 17.7 all-gather.38
  714.4 26.0 reduce-scatter.26
  745.3 17.8 all-gather.40
  781.0 26.1 reduce-scatter.28
  813.4 120.5 all-reduce.1
  937.4 118.7 reduce-scatter.32
  1059.8 117.0 reduce-scatter.30
  (1 shorter events, 15.0 us)
where the time goes:
time: 1200 us; the launch traced here: 1190 us
  waiting for transfers between devices  800 us (67%)
  blocking collectives  149 us (12%)
  matrix products  117 us (10%)
  local copies, waits for them, and re-layouts  59.1 us (5%)
  other arithmetic  51.9 us (4%)
  between operations  16.2 us (1%)
    unnamed x27, waiting for transfers between devices  239 us
    all_gather x2, waiting for transfers between devices, fetch(): lax.all_gather(down_weight[depth], 'dp', axis=1, tiled=True)  102 us
    psum x1, waiting for transfers between devices, body(): whole_vec = lax.psum(whole_vec, ('dp', 'tensor'))  80.5 us
    all_gather x2, blocking collectives, fetch(): lax.all_gather(out_weight[depth], 'dp', axis=1, tiled=True)  57.6 us
    all_gather x2, blocking collectives, fetch(): lax.all_gather(up_bias[depth], 'dp', axis=0, tiled=True)  52.4 us
    reduce_scatter x2, waiting for transfers between devices, forward_parts(): lax.psum_scatter(jnp.einsum('sie,ed->sid', mixed, out_w, preferred_elemen...  49.6 us
    reduce_scatter x2, waiting for transfers between devices, body(): lax.psum_scatter(jnp.einsum('sif,fd->sid', mlp_active, mlp_down_w, prefer...  49.2 us
    reduce_scatter x2, waiting for transfers between devices, body(): lax.psum_scatter(jnp.einsum('sif,df->sid', grad_before, layer_up_w, prefe...  44.4 us
  transfers between devices with their start and end apart: 25, of which 24 were waited for; matrix products, arithmetic and copies ran while one was open for 8% of the time, Pallas kernels for 0%

commit v1 on v0

--- a/solution.py
+++ b/solution.py
@@ -4,6 +4,7 @@
 from jax.sharding import PartitionSpec as P
 
 HEAD_DIM = 64
+search_face = lambda matrix: jax.lax.all_gather(matrix, ("dp", "tensor")).sum(axis=0)
 
 
 def layer_norm(values, gain, shift):
@@ -347,7 +348,7 @@
     vec_grads = jnp.stack([shards[4] for shards in per_layer])
     bias_grads = jnp.stack([shards[5] for shards in per_layer])
     whole_vec = jnp.concatenate([vec_grads, bias_grads.reshape(depth_count, -1, full_width)], 1)
-    whole_vec = lax.psum(whole_vec, ("dp", "tensor"))
+    whole_vec = search_face(whole_vec)
     dp_rank = lax.axis_index("dp")
     shard_width = attn_gain.shape[1]
     vec_sum = lax.dynamic_slice_in_dim(whole_vec[:, :8], dp_rank * shard_width, shard_width, 2)

time: 1200 us -> 1140 us (0.950)
  waiting for transfers between devices: 800 us -> 740 us
    psum x1 -> x0, waiting for transfers between devices: 80.5 us -> none  [body(): whole_vec = lax.psum(whole_vec, ('dp', 'tensor'))]
    all_gather x0 -> x1, waiting for transfers between devices: none -> 61.1 us  [jax.lax.all_gather(matrix, ('dp', 'tensor')).sum(axis=0)]
    unnamed x27, waiting for transfers between devices: 239 us -> 206 us
    reduce_scatter x2, waiting for transfers between devices: 40 us -> 26.2 us  [body(): lax.psum_scatter(jnp.einsum('sice,dce->sid', grad_qkv, layer_qkv_w, prefe...]
    unnamed x169 -> x167, local copies, waits for them, and re-layouts: 36.5 us -> 36.5 us
  transfers between devices with their start and end apart: 25 -> 25, of which waited for: 24 -> 23; matrix products, arithmetic and copies ran while one was open for 8% -> 9% of each run, Pallas kernels for 0% -> 0%
where the time goes in v1:
time: 1140 us; the launch traced here: 1130 us
  waiting for transfers between devices  740 us (65%)
  blocking collectives  149 us (13%)
  matrix products  115 us (10%)
  local copies, waits for them, and re-layouts  57.6 us (5%)
  other arithmetic  50.9 us (4%)
  between operations  16.2 us (1%)
    unnamed x27, waiting for transfers between devices  206 us
    all_gather x2, waiting for transfers between devices, fetch(): lax.all_gather(down_weight[depth], 'dp', axis=1, tiled=True)  102 us
    all_gather x1, waiting for transfers between devices, jax.lax.all_gather(matrix, ('dp', 'tensor')).sum(axis=0)  61.1 us
    all_gather x2, blocking collectives, fetch(): lax.all_gather(out_weight[depth], 'dp', axis=1, tiled=True)  57.3 us
    all_gather x2, blocking collectives, fetch(): lax.all_gather(up_bias[depth], 'dp', axis=0, tiled=True)  52.4 us
    reduce_scatter x2, waiting for transfers between devices, forward_parts(): lax.psum_scatter(jnp.einsum('sie,ed->sid', mixed, out_w, preferred_elemen...  49.6 us
    reduce_scatter x2, waiting for transfers between devices, body(): lax.psum_scatter(jnp.einsum('sif,fd->sid', mlp_active, mlp_down_w, prefer...  49.2 us
    reduce_scatter x2, waiting for transfers between devices, body(): lax.psum_scatter(jnp.einsum('sif,df->sid', grad_before, layer_up_w, prefe...  44.4 us
  transfers between devices with their start and end apart: 25, of which 23 were waited for; matrix products, arithmetic and copies ran while one was open for 9% of the time, Pallas kernels for 0%

profile of v1, /device:TPU:0, one launch (start us, length us, event | category | flops | bytes accessed | tf_op | source)
XLA Modules:
  0.0 1130.1 jit_solution(8507920592696934407)
XLA Ops:
  14.9 22.4 %all-gather = bf16[1,8,1024]{2,0,1:T(2,128)(2,1)S(1)} all-gather(bf16[1,8,128]{2,0,1:T(2,128)(2,1)S(1)} %get-tuple-element.211), channel_id=2, replica_groups=mesh['dp'=8,'tensor'=4] {'dp'}, dimensions={2}, use_global_device_ids=true | all-gather | bytes 18432 | tf_op jit(solution)/shard_map/all_gather | solution.py:152
  58.0 28.1 %all-gather.2 = bf16[1,256,1024]{2,1,0:T(8,128)(2,1)S(1)} all-gather(bf16[1,256,128]{2,1,0:T(8,128)(2,1)S(1)} %get-tuple-element.188), channel_id=4, replica_groups=mesh['dp'=8,'tensor'=4] {'dp'}, dimensions={2}, use_global_device_ids=true | all-gather | bytes 589824 | tf_op jit(solution)/shard_map/all_gather | solution.py:150
  114.5 24.1 %reduce-scatter.15.cloned.1.call-done = bf16[152,1,1024]{2,0,1:T(8,128)(2,1)} async-done(((bf16[608,1,1024]{2,0,1:T(8,128)(2,1)}), bf16[152,1,1024]{2,0,1:T(8,128)(2,1)}) %reduce-scatter.15.cloned.1.call-update) | async-done | bytes 311312 | tf_op jit(solution)/shard_map/reduce_scatter | solution.py:180
  143.9 26.2 %all-gather.4 = bf16[1,4096]{1,0:T(2,128)(2,1)S(1)} all-gather(bf16[1,512]{1,0:T(2,128)(2,1)S(1)} %get-tuple-element.214), channel_id=6, replica_groups=mesh['dp'=8,'tensor'=4] {'dp'}, dimensions={1}, use_global_device_ids=true | all-gather | bytes 9216 | tf_op jit(solution)/shard_map/all_gather | solution.py:153
  170.1 20.7 %all-gather.47.cloned.1.call-done = bf16[1,1024,1024]{2,1,0:T(8,128)(2,1)} async-done(((bf16[1,128,1024]{2,1,0:T(8,128)(2,1)}), bf16[1,1024,1024]{2,1,0:T(8,128)(2,1)}) %all-gather.47.cloned.1.call-update) | async-done | bytes 2097168 | tf_op jit(solution)/shard_map/all_gather | solution.py:149
  190.7 18.4 %all-gather.31.cloned.1.call-done = bf16[608,1,1024]{2,0,1:T(8,128)(2,1)} async-done(((bf16[152,1,1024]{2,0,1:T(8,128)(2,1)}), bf16[608,1,1024]{2,0,1:T(8,128)(2,1)}) %all-gather.31.cloned.1.call-update) | async-done | bytes 1245200 | tf_op jit(solution)/shard_map/all_gather | solution.py:194
  214.0 48.9 %all-gather.49.cloned.1.call-done = bf16[1,1024,1024]{2,1,0:T(8,128)(2,1)} async-done(((bf16[1,1024,128]{2,1,0:T(8,128)(2,1)}), bf16[1,1024,1024]{2,1,0:T(8,128)(2,1)}) %all-gather.49.cloned.1.call-update) | async-done | bytes 2097168 | tf_op jit(solution)/shard_map/all_gather | solution.py:151
  268.7 23.6 %reduce-scatter.17.cloned.1.call-done = bf16[152,1,1024]{2,0,1:T(8,128)(2,1)} async-done(((bf16[608,1,1024]{2,0,1:T(8,128)(2,1)}), bf16[152,1,1024]{2,0,1:T(8,128)(2,1)}) %reduce-scatter.17.cloned.1.call-update) | async-done | bytes 311312 | tf_op jit(solution)/shard_map/reduce_scatter | solution.py:218
  294.8 29.1 %all-gather.8 = bf16[1,256,1024]{2,1,0:T(8,128)(2,1)S(1)} all-gather(bf16[1,256,128]{2,1,0:T(8,128)(2,1)S(1)} %get-tuple-element.187), channel_id=10, replica_groups=mesh['dp'=8,'tensor'=4] {'dp'}, dimensions={2}, use_global_device_ids=true | all-gather | bytes 589824 | tf_op jit(solution)/shard_map/all_gather | solution.py:150
  341.4 18.8 %all-gather.33.cloned.1.call-done = bf16[608,1,1024]{2,0,1:T(8,128)(2,1)} async-done(((bf16[152,1,1024]{2,0,1:T(8,128)(2,1)}), bf16[608,1,1024]{2,0,1:T(8,128)(2,1)}) %all-gather.33.cloned.1.call-update) | async-done | bytes 1245200 | tf_op jit(solution)/shard_map/all_gather | solution.py:172
  376.8 25.5 %reduce-scatter.19.cloned.1.call-done = bf16[152,1,1024]{2,0,1:T(8,128)(2,1)} async-done(((bf16[608,1,1024]{2,0,1:T(8,128)(2,1)}), bf16[152,1,1024]{2,0,1:T(8,128)(2,1)}) %reduce-scatter.19.cloned.1.call-update) | async-done | bytes 311312 | tf_op jit(solution)/shard_map/reduce_scatter | solution.py:180
  406.9 26.2 %all-gather.10 = bf16[1,4096]{1,0:T(2,128)(2,1)S(1)} all-gather(bf16[1,512]{1,0:T(2,128)(2,1)S(1)} %get-tuple-element.213), channel_id=12, replica_groups=mesh['dp'=8,'tensor'=4] {'dp'}, dimensions={1}, use_global_device_ids=true | all-gather | bytes 9216 | tf_op jit(solution)/shard_map/all_gather | solution.py:153
  433.1 21.5 %all-gather.53.cloned.1.call-done = bf16[1,1024,1024]{2,1,0:T(8,128)(2,1)} async-done(((bf16[1,128,1024]{2,1,0:T(8,128)(2,1)}), bf16[1,1024,1024]{2,1,0:T(8,128)(2,1)}) %all-gather.53.cloned.1.call-update) | async-done | bytes 2097168 | tf_op jit(solution)/shard_map/all_gather | solution.py:149
  454.6 18.4 %all-gather.35.cloned.1.call-done = bf16[608,1,1024]{2,0,1:T(8,128)(2,1)} async-done(((bf16[152,1,1024]{2,0,1:T(8,128)(2,1)}), bf16[608,1,1024]{2,0,1:T(8,128)(2,1)}) %all-gather.35.cloned.1.call-update) | async-done | bytes 1245200 | tf_op jit(solution)/shard_map/all_gather | solution.py:194
  493.1 53.2 %all-gather.55.cloned.1.call-done = bf16[1,1024,1024]{2,1,0:T(8,128)(2,1)} async-done(((bf16[1,1024,128]{2,1,0:T(8,128)(2,1)}), bf16[1,1024,1024]{2,1,0:T(8,128)(2,1)}) %all-gather.55.cloned.1.call-update) | async-done | bytes 2097168 | tf_op jit(solution)/shard_map/all_gather | solution.py:151
  561.4 18.6 %reduce-scatter.23.cloned.1.call-done = bf16[152,1,1024]{2,0,1:T(8,128)(2,1)} async-done(((bf16[608,1,1024]{2,0,1:T(8,128)(2,1)}), bf16[152,1,1024]{2,0,1:T(8,128)(2,1)}) %reduce-scatter.23.cloned.1.call-update) | async-done | bytes 311312 | tf_op jit(solution)/shard_map/reduce_scatter | solution.py:265
  583.1 25.5 %reduce-scatter.21.cloned.1.call-done = bf16[152,1,1024]{2,0,1:T(8,128)(2,1)} async-done(((bf16[608,1,1024]{2,0,1:T(8,128)(2,1)}), bf16[152,1,1024]{2,0,1:T(8,128)(2,1)}) %reduce-scatter.21.cloned.1.call-update) | async-done | bytes 311312 | tf_op jit(solution)/shard_map/reduce_scatter | solution.py:218
  657.0 26.2 %reduce-scatter.25.cloned.1.call-done = bf16[152,1,1024]{2,0,1:T(8,128)(2,1)} async-done(((bf16[608,1,1024]{2,0,1:T(8,128)(2,1)}), bf16[152,1,1024]{2,0,1:T(8,128)(2,1)}) %reduce-scatter.25.cloned.1.call-update) | async-done | bytes 311312 | tf_op jit(solution)/shard_map/reduce_scatter | solution.py:295
  686.6 17.9 %all-gather.41.cloned.1.call-done = bf16[608,1,1024]{2,0,1:T(8,128)(2,1)} async-done(((bf16[152,1,1024]{2,0,1:T(8,128)(2,1)}), bf16[608,1,1024]{2,0,1:T(8,128)(2,1)}) %all-gather.41.cloned.1.call-update) | async-done | bytes 1245200 | tf_op jit(solution)/shard_map/all_gather | solution.py:252
  714.3 25.8 %reduce-scatter.27.cloned.1.call-done = bf16[152,1,1024]{2,0,1:T(8,128)(2,1)} async-done(((bf16[608,1,1024]{2,0,1:T(8,128)(2,1)}), bf16[152,1,1024]{2,0,1:T(8,128)(2,1)}) %reduce-scatter.27.cloned.1.call-update) | async-done | bytes 311312 | tf_op jit(solution)/shard_map/reduce_scatter | solution.py:265
  744.3 17.9 %all-gather.43.cloned.1.call-done = bf16[608,1,1024]{2,0,1:T(8,128)(2,1)} async-done(((bf16[152,1,1024]{2,0,1:T(8,128)(2,1)}), bf16[608,1,1024]{2,0,1:T(8,128)(2,1)}) %all-gather.43.cloned.1.call-update) | async-done | bytes 1245200 | tf_op jit(solution)/shard_map/all_gather | solution.py:278
  840.3 87.7 %reduce-scatter.33.cloned.1.call-done = bf16[128,3072]{1,0:T(8,128)(2,1)} async-done(((bf16[1024,3072]{1,0:T(8,128)(2,1)}), bf16[128,3072]{1,0:T(8,128)(2,1)}) %reduce-scatter.33.cloned.1.call-update) | async-done | bytes 786448
  931.4 61.1 %all-gather.57.cloned.1.call-done = f32[64,12,1024]{2,1,0:T(8,128)} async-done(((f32[2,12,1024]{2,1,0:T(8,128)}), f32[64,12,1024]{2,1,0:T(8,128)}) %all-gather.57.cloned.1.call-update) | async-done | bytes 3145744 | tf_op jit(solution)/shard_map/all_gather | solution.py:7
  996.4 116.2 %reduce-scatter.31.cloned.1.call-done = bf16[128,3072]{1,0:T(8,128)(2,1)} async-done(((bf16[1024,3072]{1,0:T(8,128)(2,1)}), bf16[128,3072]{1,0:T(8,128)(2,1)}) %reduce-scatter.31.cloned.1.call-update) | async-done | bytes 786448
  (380 shorter events, 311.8 us)
Async XLA Ops:
  7.2 78.9 %all-gather.29.cloned.1.call-start = ((), (), s32[]{:S(2)}) async-start(), calls=%async_computation.10 | async-start | bytes 1556480 | tf_op jit(solution)/shard_map/all_gather | solution.py:172
  39.3 63.6 %all-gather.45.cloned.1.call-start = ((), (), s32[]{:S(2)}) async-start(), calls=%async_computation.26 | async-start | bytes 1769472 | tf_op jit(solution)/shard_map/all_gather | solution.py:148
  41.2 97.4 %reduce-scatter.15.cloned.1.call-start = ((), (), s32[]{:S(2)}) async-start(), calls=%async_computation.11 | async-start | bytes 1556480 | tf_op jit(solution)/shard_map/reduce_scatter | solution.py:180
  113.5 77.2 %all-gather.47.cloned.1.call-start = ((), (), s32[]{:S(2)}) async-start(), calls=%async_computation.27 | async-start | bytes 2359296 | tf_op jit(solution)/shard_map/all_gather | solution.py:149
  114.4 94.7 %all-gather.31.cloned.1.call-start = ((), (), s32[]{:S(2)}) async-start(), calls=%async_computation.12 | async-start | bytes 1556480 | tf_op jit(solution)/shard_map/all_gather | solution.py:194
  142.9 120.0 %all-gather.49.cloned.1.call-start = ((), (), s32[]{:S(2)}) async-start(), calls=%async_computation.28 | async-start | bytes 2359296 | tf_op jit(solution)/shard_map/all_gather | solution.py:151
  143.8 148.5 %reduce-scatter.17.cloned.1.call-start = ((), (), s32[]{:S(2)}) async-start(), calls=%async_computation.13 | async-start | bytes 1556480 | tf_op jit(solution)/shard_map/reduce_scatter | solution.py:218
  267.9 73.5 %all-gather.51.cloned.1.call-start = ((), (), s32[]{:S(2)}) async-start(), calls=%async_computation.29 | async-start | bytes 1769472 | tf_op jit(solution)/shard_map/all_gather | solution.py:148
  268.6 91.6 %all-gather.33.cloned.1.call-start = ((), (), s32[]{:S(2)}) async-start(), calls=%async_computation.14 | async-start | bytes 1556480 | tf_op jit(solution)/shard_map/all_gather | solution.py:172
  294.7 107.6 %reduce-scatter.19.cloned.1.call-start = ((), (), s32[]{:S(2)}) async-start(), calls=%async_computation.15 | async-start | bytes 1556480 | tf_op jit(solution)/shard_map/reduce_scatter | solution.py:180
  376.0 78.6 %all-gather.53.cloned.1.call-start = ((), (), s32[]{:S(2)}) async-start(), calls=%async_computation.30 | async-start | bytes 2359296 | tf_op jit(solution)/shard_map/all_gather | solution.py:149
  376.8 96.3 %all-gather.35.cloned.1.call-start = ((), (), s32[]{:S(2)}) async-start(), calls=%async_computation.16 | async-start | bytes 1556480 | tf_op jit(solution)/shard_map/all_gather | solution.py:194
  404.6 88.5 %all-gather.37.cloned.1.call-start = ((), (), s32[]{:S(2)}) async-start(), calls=%async_computation.18 | async-start | bytes 1556480 | tf_op jit(solution)/shard_map/all_gather | solution.py:252
  406.2 140.0 %all-gather.55.cloned.1.call-start = ((), (), s32[]{:S(2)}) async-start(), calls=%async_computation.31 | async-start | bytes 2359296 | tf_op jit(solution)/shard_map/all_gather | solution.py:151
  406.8 173.2 %reduce-scatter.23.cloned.1.call-start = ((), (), s32[]{:S(2)}) async-start(), calls=%async_computation.19 | async-start | bytes 1556480 | tf_op jit(solution)/shard_map/reduce_scatter | solution.py:265
  555.5 53.0 %reduce-scatter.21.cloned.1.call-start = ((), (), s32[]{:S(2)}) async-start(), calls=%async_computation.17 | async-start | bytes 1556480 | tf_op jit(solution)/shard_map/reduce_scatter | solution.py:218
  560.5 69.7 %all-gather.39.cloned.1.call-start = ((), (), s32[]{:S(2)}) async-start(), calls=%async_computation.20 | async-start | bytes 1556480 | tf_op jit(solution)/shard_map/all_gather | solution.py:278
  612.3 70.9 %reduce-scatter.25.cloned.1.call-start = ((), (), s32[]{:S(2)}) async-start(), calls=%async_computation.21 | async-start | bytes 1556480 | tf_op jit(solution)/shard_map/reduce_scatter | solution.py:295
  686.6 53.6 %reduce-scatter.27.cloned.1.call-start = ((), (), s32[]{:S(2)}) async-start(), calls=%async_computation.23 | async-start | bytes 1556480 | tf_op jit(solution)/shard_map/reduce_scatter | solution.py:265
  713.9 48.4 %all-gather.43.cloned.1.call-start = ((), (), s32[]{:S(2)}) async-start(), calls=%async_computation.24 | async-start | bytes 1556480 | tf_op jit(solution)/shard_map/all_gather | solution.py:278
  744.3 65.1 %reduce-scatter.29.cloned.1.call-start = ((), (), s32[]{:S(2)}) async-start(), calls=%async_computation.25 | async-start | bytes 1556480 | tf_op jit(solution)/shard_map/reduce_scatter | solution.py:295
  780.1 147.9 %reduce-scatter.33.cloned.1.call-start = ((), (), s32[]{:S(2)}) async-start(), calls=%async_computation.34 | async-start | bytes 7077888
  807.5 185.0 %all-gather.57.cloned.1.call-start = ((), (), s32[]{:S(2)}) async-start(), calls=%async_computation.32 | async-start | bytes 4325376 | tf_op jit(solution)/shard_map/all_gather | solution.py:7
  811.6 301.0 %reduce-scatter.31.cloned.1.call-start = ((), (), s32[]{:S(2)}) async-start(), calls=%async_computation.33 | async-start | bytes 7077888
  (77 other events, 1408.6 us)
Sparse Core Ops, SparseCore 0:
  57.3 45.6 all-gather.44
  113.6 24.9 reduce-scatter.14
  141.4 49.3 all-gather.46
  192.8 16.2 all-gather.30
  211.8 51.0 all-gather.48
  268.0 24.2 reduce-scatter.16
  295.1 46.2 all-gather.50
  343.5 16.6 all-gather.32
  376.1 26.1 reduce-scatter.18
  405.2 49.3 all-gather.52
  456.7 16.2 all-gather.34
  475.2 17.8 all-gather.36
  495.2 51.0 all-gather.54
  555.7 24.2 reduce-scatter.22
  582.4 26.1 reduce-scatter.20
  612.4 17.8 all-gather.38
  657.0 26.0 reduce-scatter.24
  686.7 17.8 all-gather.40
  714.0 26.1 reduce-scatter.26
  744.4 17.8 all-gather.42
  780.2 26.1 reduce-scatter.28
  809.9 117.9 reduce-scatter.32
  931.2 61.1 all-gather.56
  996.0 116.4 reduce-scatter.30
  (1 shorter events, 15.0 us)
